TPU v7x, 32 devices: a whole 2x2x4 slice. The times are simulated.
32 devices in a mesh: ny: 4 (over x, core), nx: 8 (over z, y).
Axes of the slice: x: 2, y: 2, z: 4, core: 2. Of those that a mesh axis runs over, the one named last changes fastest.
Arguments:
- elevation: float32 [576, 9216], P('ny', 'nx'), may hold values from -6 to 6
- flux_x: float32 [576, 9216], P('ny', 'nx'), may hold values from -3 to 3
- flux_y: float32 [576, 9216], P('ny', 'nx'), may hold values from -3 to 3
- depth: float32 [576, 9216], P('ny', 'nx'), may hold values from 0.5 to 2
- wet_mask: int32 [4, 576, 9216], P(None, 'ny', 'nx'), may hold values 0 or 1
- shifts: int32 [4, 2], replicated, may hold values from 0 to 9, as said below
- parent_vals: float32 [4, 8192, 128], P(None, ('ny', 'nx')), may hold values from -3 to 3
- row_dest: int32 [4, 8192], P(None, ('ny', 'nx')), may hold values from 0 to 31, as said below
- row_coarse: int32 [4, 8192], P(None, ('ny', 'nx')), may hold values from 0 to 15
- edge_owner: int32 [4, 4], P(None, 'ny'), may hold values from 0 to 7
- edge_panels: float32 [4, 8, 576], P(None, 'nx', 'ny'), may hold values from -8 to 8
Outputs:
- elevation_out: float32 [576, 9216], P('ny', 'nx')
- flux_x_out: float32 [576, 9216], P('ny', 'nx')
- flux_y_out: float32 [576, 9216], P('ny', 'nx')
Inputs may be any that keep to these rules, and one draw needn't show every extreme that they name: In every draw some step shifts the rows by 9 and some step shifts the columns by 9. `row_dest`: in each step, of the 256 rows of one device at most 8 name any one owner; in each step one owner is named by exactly 8 rows of every device.
All inputs are finite; a program needn't handle non-finite values. No bound on the sum of `wet_mask` on one device may be relied on, other than what follows from the above.
Results may differ from a plain program's by a relative error of at most 0.00014.
Values sent between devices are 32-bit elements; how exact they have to be, the bound alone decides.
A program may use at most 128 MiB of HBM per device.

v0:
```python
import functools

import jax
import jax.numpy as jnp
from jax import lax
from jax.experimental import pallas as pl
from jax.experimental.pallas import tpu as pltpu
from jax.sharding import PartitionSpec as P

RATIO = 9
STEPS = 4
SH = 9
CAP = 8
PAD = 8
LANES = 128
MESH = pl.DeviceIdType.MESH
F32 = jnp.float32
BF16 = jnp.bfloat16
I32 = jnp.int32

STATE_HI = STEPS * (SH + 1)
WET_HI = [SH * (STEPS - 1 - s) + STEPS - s for s in range(STEPS)]
WET_LO = [STEPS - s for s in range(STEPS)]
AUX_HI = [WET_HI[0]] + WET_HI
AUX_LO = [WET_LO[0]] + WET_LO


def starts(widths):
    return [sum(widths[:k]) for k in range(len(widths))]


def round_up(value, unit):
    return -(-value // unit) * unit


def pieces(value):
    high = value.astype(BF16)
    rest = value - high.astype(F32)
    mid = rest.astype(BF16)
    low = (rest - mid.astype(F32)).astype(BF16)
    return high, mid, low


def iota(shape, dim):
    return lax.broadcasted_iota(I32, shape, dim)


def prep_kernel(owners, dest, coarse, vals, e, u, v, d_0, d_1, w_0, w_1, eowner, epanel,
                send, tgt, hi, lo, edge):
    depth, wet = (d_0, d_1), (w_0, w_1)
    rows = dest.shape[1]
    places = owners * CAP
    before = (iota((rows, rows), 0) < iota((rows, rows), 1)).astype(BF16)
    targets = jnp.zeros((owners, LANES), F32)
    for s in range(STEPS):
        d = dest[s : s + 1, :]
        hits = iota((owners, rows), 0) == d
        hits_f = hits.astype(F32)
        earlier = jnp.dot(hits.astype(BF16), before, preferred_element_type=F32)
        rank = jnp.sum(hits_f * earlier, axis=0, keepdims=True).astype(I32)
        place = d * CAP + rank
        pick = (iota((places, rows), 0) == place).astype(BF16)
        total = jnp.zeros((places, vals.shape[2]), F32)
        for piece in pieces(vals[s]):
            total = total + jnp.dot(pick, piece, preferred_element_type=F32)
        send[:, s * CAP : (s + 1) * CAP, :] = total.reshape(owners, CAP, vals.shape[2])
        lane_pick = (iota((LANES, rows), 0) == rank + s * CAP).astype(BF16)
        named = (hits_f * (coarse[s : s + 1, :] + 1).astype(F32)).astype(BF16)
        targets = targets + lax.dot_general(
            named, lane_pick, (((1,), (1,)), ((), ())), preferred_element_type=F32
        )
    for o in range(owners):
        tgt[o] = targets[o : o + 1, :]
    cy = e.shape[0]
    lane = iota((cy, LANES), 1)

    def put(base, tile, at, width):
        moved = pltpu.roll(tile, at % LANES, 1) if at % LANES else tile
        return jnp.where((lane >= at) & (lane < at + width), moved, base)

    first = e[...]
    for k, ref in ((1, u), (2, v)):
        first = put(first, ref[...], k * STATE_HI, STATE_HI)
    hi[:, :LANES] = first
    second = depth[0][...]
    last = jnp.zeros((cy, LANES), F32)
    for k in range(STEPS + 1):
        if k:
            second = put(second, wet[0][k - 1].astype(F32), starts(AUX_HI)[k], AUX_HI[k])
        tile = wet[1][k - 1].astype(F32) if k else depth[1][...]
        at = starts(AUX_LO)[k]
        moved = pltpu.roll(tile, (at + AUX_LO[k]) % LANES, 1)
        last = jnp.where((lane >= at) & (lane < at + AUX_LO[k]), moved, last)
    hi[:, LANES:] = second
    lo[...] = last
    mine = eowner[...] == lax.axis_index("nx")
    edge[...] = jnp.where(mine, epanel[:, 0, :], 0.0)


def comm_kernel(ny, nx, n_halo, send, tgt, e, u, v, depth, wet, hi_p, lo_p, edge_p,
                srs, srd, srw0, srw1, srw2, srw3, nrd, nrw, hi, lo, fc, edges,
                got, got_t, own, a_ssem, a_rsem, h_ssem, h_rsem, f_ssem, f_rsem,
                e_ssem, e_rsem, l_sem):
    y, x = lax.axis_index("ny"), lax.axis_index("nx")
    owners = ny * nx
    me = y * nx + x
    cy = e.shape[0]

    def remote(src, dst, ss, rs, ty, tx):
        return pltpu.make_async_remote_copy(
            src_ref=src, dst_ref=dst, send_sem=ss, recv_sem=rs,
            device_id=(ty, tx), device_id_type=MESH)

    def to_owner(k):
        t = lax.rem(me + k, owners)
        ty, tx = t // nx, lax.rem(t, nx)
        return (remote(send.at[t], got.at[me], a_ssem.at[0], a_rsem.at[0], ty, tx),
                remote(tgt.at[t], got_t.at[me], a_ssem.at[1], a_rsem.at[1], ty, tx))

    def start_owner(k, carry):
        for copy in to_owner(k):
            copy.start()
        return carry

    lax.fori_loop(1, owners, start_owner, 0)
    self_v = pltpu.make_async_copy(send.at[me], got.at[me], a_rsem.at[0])
    self_t = pltpu.make_async_copy(tgt.at[me], got_t.at[me], a_rsem.at[1])
    self_v.start()
    self_t.start()

    def sends_to(dy, dx):
        terms = []
        if dy:
            terms.append(y > 0 if dy < 0 else y < ny - 1)
        if dx:
            terms.append(x > 0 if dx < 0 else x < nx - 1)
        return functools.reduce(jnp.logical_and, terms)

    wet_rows = [srw0, srw1, srw2, srw3]
    plan = [(-1, 0, ref.at[pl.ds(0, STATE_HI)], srs.at[k]) for k, ref in enumerate((e, u, v))]
    plan.append((-1, 0, depth.at[pl.ds(0, srd.shape[0])], srd))
    for s in range(STEPS):
        plan.append((-1, 0, wet.at[s, pl.ds(0, wet_rows[s].shape[0])], wet_rows[s]))
    end = pl.ds(cy - PAD, PAD)
    plan.append((1, 0, depth.at[end], nrd))
    plan.append((1, 0, wet.at[:, end], nrw))
    low_rows = lo.shape[0] - PAD - cy
    plan.append((0, -1, hi_p, hi.at[pl.ds(PAD, cy)]))
    plan.append((0, 1, lo_p, lo.at[pl.ds(PAD, cy)]))
    plan.append((-1, -1, hi_p.at[pl.ds(0, STATE_HI)], hi.at[pl.ds(PAD + cy, STATE_HI)]))
    plan.append((1, -1, hi_p.at[end], hi.at[pl.ds(0, PAD)]))
    plan.append((-1, 1, lo_p.at[pl.ds(0, low_rows)], lo.at[pl.ds(PAD + cy, low_rows)]))
    plan.append((1, 1, lo_p.at[end], lo.at[pl.ds(0, PAD)]))
    assert len(plan) == n_halo
    halos = []
    for k, (dy, dx, src, dst) in enumerate(plan):
        copy = remote(src, dst, h_ssem.at[k], h_rsem.at[k], y + dy, x + dx)
        halos.append((copy, dy, dx))
        pl.when(sends_to(dy, dx))(copy.start)

    for dy in (-1, 0, 1):
        copy = remote(edge_p, edges.at[1 - dy, x], e_ssem.at[1 - dy], e_rsem.at[1 - dy],
                      y + dy, x * 0)
        there = (x > 0) if dy == 0 else sends_to(dy, 0)
        pl.when(there)(copy.start)
    self_e = pltpu.make_async_copy(edge_p, edges.at[1, 0], e_rsem.at[1])
    pl.when(x == 0)(self_e.start)

    pltpu.make_async_copy(got, got, a_rsem.at[0]).wait()
    pltpu.make_async_copy(got_t, got_t, a_rsem.at[1]).wait()
    n_coarse, n_cols = own.shape[1], own.shape[2]
    places = owners * CAP
    named = got_t[:, 0, :].astype(BF16)
    place_owner = iota((owners, places), 1) // CAP
    own_place = place_owner == iota((owners, places), 0)
    slot = iota((LANES, places), 1) - iota((LANES, places), 1) // CAP * CAP
    for s in range(STEPS):
        spread = (iota((LANES, places), 0) == slot + s * CAP).astype(BF16)
        wide = jnp.dot(named, spread, preferred_element_type=F32)
        target = jnp.sum(jnp.where(own_place, wide, 0.0), axis=0, keepdims=True)
        pick = (iota((n_coarse, places), 0).astype(F32) == target - 1.0).astype(BF16)
        values = got[:, s * CAP : (s + 1) * CAP, :].reshape(places, n_cols)
        total = jnp.zeros((n_coarse, n_cols), F32)
        for piece in pieces(values):
            total = total + jnp.dot(pick, piece, preferred_element_type=F32)
        own[s] = total
    half = n_coarse // 2
    self_f = pltpu.make_async_copy(own, fc.at[4], l_sem.at[0])
    self_f.start()
    coarse = []
    for dy in (-1, 0, 1):
        for dx in (-1, 0, 1):
            if dy == 0 and dx == 0:
                continue
            k = (1 - dy) * 3 + (1 - dx)
            part = {-1: pl.ds(0, half), 0: pl.ds(0, n_coarse), 1: pl.ds(half, half)}[dy]
            copy = remote(own.at[:, part], fc.at[k, :, part], f_ssem.at[k], f_rsem.at[k],
                          y + dy, x + dx)
            coarse.append((copy, dy, dx))
            pl.when(sends_to(dy, dx))(copy.start)
    for copy, dy, dx in halos + coarse:
        pl.when(sends_to(-dy, -dx))(copy.wait_recv)
    for dy in (-1, 0, 1):
        whole = edges.at[1 - dy]
        here = (x == 0) if dy == 0 else jnp.logical_and(x == 0, sends_to(-dy, 0))
        pl.when(here)(pltpu.make_async_copy(whole, whole, e_rsem.at[1 - dy]).wait)
    for copy, dy, dx in halos + coarse:
        pl.when(sends_to(dy, dx))(copy.wait_send)
    for dy in (-1, 0, 1):
        copy = remote(edge_p, edges.at[1 - dy, x], e_ssem.at[1 - dy], e_rsem.at[1 - dy],
                      y + dy, x * 0)
        there = (x > 0) if dy == 0 else sends_to(dy, 0)
        pl.when(there)(copy.wait_send)
    self_f.wait()

    def end_owner(k, carry):
        for copy in to_owner(k):
            copy.wait_send()
        return carry

    lax.fori_loop(1, owners, end_owner, 0)


def step_kernel(ny, nx, shifts, e, u, v, depth, wet, srs, srd, srw0, srw1, srw2, srw3,
                nrd, nrw, hi, lo, fc, edges, out_e, out_u, out_v,
                ext, ext_d, ext_w, hi_v, lo_v, edge_v, fc_v, work, cur, force, sems):
    y, x = lax.axis_index("ny"), lax.axis_index("nx")
    cy, cx = e.shape
    width = ext.shape[2]
    win = cur.shape[1]
    halo = srs.shape[1]
    own_cols = pl.ds(0, cx)
    groups = [[], [], [], [], [], []]
    groups[0] += [(hi, hi_v), (lo, lo_v), (fc, fc_v), (edges, edge_v)]
    for k, ref in enumerate((e, u, v)):
        groups[1].append((ref, ext.at[k, pl.ds(0, cy), own_cols]))
        groups[1].append((srs.at[k], ext.at[k, pl.ds(cy, halo), own_cols]))
    groups[1].append((nrd, ext_d.at[pl.ds(0, PAD), own_cols]))
    groups[1].append((depth, ext_d.at[pl.ds(PAD, cy), own_cols]))
    groups[1].append((srd, ext_d.at[pl.ds(PAD + cy, srd.shape[0]), own_cols]))
    for s, rows in enumerate((srw0, srw1, srw2, srw3)):
        groups[2 + s].append((nrw.at[s], ext_w.at[s, pl.ds(0, PAD), own_cols]))
        groups[2 + s].append((wet.at[s], ext_w.at[s, pl.ds(PAD, cy), own_cols]))
        groups[2 + s].append((rows, ext_w.at[s, pl.ds(PAD + cy, rows.shape[0]), own_cols]))
    copies = []
    count = 0
    for group in groups:
        made = []
        for src, dst in group:
            made.append(pltpu.make_async_copy(src, dst, sems.at[count]))
            made[-1].start()
            count += 1
        copies.append(made)

    def finish(group):
        for copy in copies[group]:
            copy.wait()

    sum_r = [sum([shifts[t, 0] for t in range(s, STEPS)], jnp.int32(0)) for s in range(STEPS + 1)]
    sum_c = [sum([shifts[t, 1] for t in range(s, STEPS)], jnp.int32(0)) for s in range(STEPS + 1)]

    finish(0)
    n_coarse, n_cols = fc.shape[2], fc.shape[3]
    has_y = {-1: y > 0, 0: y >= 0, 1: y < ny - 1}
    has_x = {-1: x > 0, 0: x >= 0, 1: x < nx - 1}
    half = n_coarse // 2

    def weights(fine, which, at, fine_count, coarse_count):
        inner = fine - which * fine_count
        spot = jnp.clip(2 * inner + 1 - RATIO, 0, 2 * RATIO * (coarse_count - 1))
        weight = jnp.maximum(2 * RATIO - jnp.abs(spot - 2 * RATIO * at), 0)
        inside = (inner >= 0) & (inner < fine_count)
        return jnp.where(inside, weight, 0).astype(F32).astype(BF16)

    lane_e = iota((n_coarse, n_cols), 1)
    row_e = iota((n_coarse, n_cols), 0)

    def forcing(s):
        q = iota((win, 3 * n_coarse), 1)
        which = (q >= n_coarse).astype(I32) + (q >= 2 * n_coarse).astype(I32) - 1
        fine = iota((win, 3 * n_coarse), 0) - PAD + sum_r[s + 1]
        row_w = weights(fine, which, q - (which + 1) * n_coarse, cy, n_coarse)
        bands = []
        for dy in (-1, 0, 1):
            sides = {}
            for dx in (-1, 0, 1):
                ok = has_y[dy] & has_x[dx]
                block = fc_v[(dy + 1) * 3 + dx + 1, s]
                if dy:
                    ok = ok & ((row_e >= half) if dy < 0 else (row_e < half))
                sides[dx] = jnp.where(ok, block, 0.0)
            beside = jnp.where(lane_e < n_cols // 2, sides[1], sides[-1])
            bands.append(jnp.concatenate([sides[0], beside], axis=1))
        coarse = jnp.concatenate(bands, axis=0)
        section = jnp.zeros((win, 2 * n_cols), F32)
        for piece in pieces(coarse):
            section = section + jnp.dot(row_w, piece, preferred_element_type=F32)
        q = iota((2 * n_cols, width), 0)
        at = q - jnp.where(q >= n_cols, n_cols, 0)
        which = jnp.where(q < n_cols, 0, jnp.where(at < n_cols // 2, 1, -1))
        lane = iota((2 * n_cols, width), 1)
        fine = lane - jnp.where(lane >= width - PAD, width, 0) + sum_c[s + 1]
        col_w = weights(fine, which, at, cx, n_cols)
        total = jnp.zeros((win, width), F32)
        for piece in pieces(section):
            total = total + jnp.dot(piece, col_w, preferred_element_type=F32)
        force[...] = total * (1.0 / (4.0 * RATIO * RATIO))

    rows_here = hi_v.shape[0]
    lane_t = iota((rows_here, LANES), 1)

    def moved(tile, by):
        by = by % LANES
        return pltpu.roll(tile, by, 1) if by else tile

    for k in range(3):
        ext[k, pl.ds(0, cy + halo), cx : cx + LANES] = moved(
            hi_v[pl.ds(PAD, cy + halo), :LANES], -k * STATE_HI)
    high = hi_v[:, LANES:]
    for k in range(STEPS + 1):
        high_k = moved(high, -starts(AUX_HI)[k])
        low_k = moved(lo_v[...], -(starts(AUX_LO)[k] + AUX_LO[k]))
        tile = jnp.where(lane_t < LANES // 2, high_k, low_k)
        if k == 0:
            ext_d[pl.ds(0, rows_here), cx : cx + LANES] = tile
        else:
            ext_w[k - 1, pl.ds(0, rows_here), cx : cx + LANES] = tile.astype(I32)

    def rows_at(load, start):
        base = pl.multiple_of(start // PAD * PAD, PAD)
        both = load(pl.ds(base, 2 * PAD))
        return pltpu.roll(both, lax.rem(2 * PAD - (start - base), 2 * PAD), 0)[:PAD]

    lane = iota((PAD, width), 1)
    row = iota((PAD, width), 0)
    row_1 = iota((PAD, 1), 0)
    col_local = lane - jnp.where(lane >= width - PAD, width, 0)
    edge_sum = jnp.sum(edge_v[...], axis=1)

    for s in range(STEPS):
        forcing(s)
        if s == 0:
            finish(1)
        finish(2 + s)
        off_r, off_c = sum_r[s + 1], sum_c[s + 1]
        gcol = col_local + (x * cx + off_c)
        col_in = (gcol >= 0) & (gcol < nx * cx)
        col_ok = col_in & (gcol + shifts[s, 1] < nx * cx)
        ghost_col = gcol == -1
        back = lax.rem(width - off_c, width)
        back_0 = lax.rem(width - sum_c[0], width)
        edge_rows = [edge_sum[d, s : s + 1, :] for d in range(3)]

        def fill(t, carry):
            a = pl.multiple_of(t * PAD, PAD)
            local = row + (a - PAD) + off_r
            grow = local + y * cy
            row_in = (grow >= 0) & (grow < ny * cy)
            inside = row_in & col_in
            valid = row_in & col_ok & (grow + shifts[s, 0] < ny * cy)
            fields = []
            for k in range(3):
                if s == 0:
                    piece = rows_at(lambda at: ext[k, at, :], a - PAD + sum_r[0])
                    piece = pltpu.roll(piece, back_0, 1)
                else:
                    piece = cur[k, pl.ds(a, PAD), :]
                fields.append(jnp.where(valid, piece, 0.0))
            surface = jnp.where(inside, fields[0] + force[pl.ds(a, PAD), :], 0.0)
            mask = rows_at(lambda at: ext_w[s, at, :], a + off_r)
            mask = jnp.where(inside, pltpu.roll(mask, back, 1).astype(F32), 0.0)
            bed = rows_at(lambda at: ext_d[at, :], a + off_r)
            bed = jnp.where(inside, pltpu.roll(bed, back, 1), 0.0)
            spot = row_1 + (a - PAD) + off_r
            value = jnp.zeros((PAD, 1), F32)
            for d in range(3):
                at = iota((PAD, cy), 1) + (d - 1) * cy
                value = value + jnp.sum(
                    jnp.where(at == spot, edge_rows[d], 0.0), axis=1, keepdims=True)
            ghost = ghost_col & row_in
            surface = jnp.where(ghost, value, surface)
            mask = jnp.where(ghost, 1.0, mask)
            for k, field in enumerate((surface, fields[1], fields[2], mask, bed)):
                work[k, pl.ds(a + PAD, PAD), :] = field
            return carry

        lax.fori_loop(0, win // PAD, fill, 0)

        def advance(t, carry):
            a = pl.multiple_of(t * PAD, PAD)
            around = [work[k, pl.ds(a, 3 * PAD), :] for k in range(5)]
            here = [f[PAD : 2 * PAD] for f in around]

            def faces(low, up, normal, cross):
                e_l, m_l, b_l = low[0], low[3], low[4]
                e_h, m_h, b_h = up[0], up[3], up[4]
                opened = m_l * m_h
                thin = 0.25 * opened
                rise = e_h - e_l
                level = e_h + e_l
                n_l, n_h = low[normal], up[normal]
                mass = thin * (2.0 * (n_l + n_h) - rise)
                push = thin * ((b_l + b_h) * level - (n_h - n_l))
                shear = thin * (low[cross] - up[cross])
                return mass, push, shear

            east = [pltpu.roll(f, width - 1, 1) for f in here]
            flux = faces(here, east, 1, 2)
            total = [f - pltpu.roll(f, 1, 1) for f in flux]
            upper = [f[PAD + 1 : 2 * PAD + 1] for f in around]
            lower = [f[PAD - 1 : 2 * PAD - 1] for f in around]
            f_n = faces(here, upper, 2, 1)
            f_s = faces(lower, here, 2, 1)
            d_mass, d_push, d_shear = [p - q for p, q in zip(f_n, f_s)]
            new = (
                here[0] - 0.25 * (total[0] + d_mass),
                here[3] * (here[1] - 0.25 * (total[1] + d_shear)),
                here[3] * (here[2] - 0.25 * (total[2] + d_push)),
            )
            for k in range(3):
                if s == STEPS - 1:
                    (out_e, out_u, out_v)[k][pl.ds(pl.multiple_of(a - PAD, PAD), PAD), :] = new[k][:, :cx]
                else:
                    cur[k, pl.ds(a, PAD), :] = new[k]
            return carry

        if s == STEPS - 1:
            lax.fori_loop(1, 1 + cy // PAD, advance, 0)
        else:
            lax.fori_loop(0, win // PAD, advance, 0)


def local(elevation, flux_x, flux_y, depth, wet_mask, shifts, parent_vals, row_dest, row_coarse,
          edge_owner, edge_panels):
    cy, cx = elevation.shape
    ny, nx = lax.axis_size("ny"), lax.axis_size("nx")
    owners = ny * nx
    n_cols = parent_vals.shape[2]
    n_coarse = cy // RATIO
    sds = jax.ShapeDtypeStruct
    any_ = pl.BlockSpec(memory_space=pl.ANY)
    vm = pl.BlockSpec(memory_space=pltpu.VMEM)
    sm = pl.BlockSpec(memory_space=pltpu.SMEM)

    def whole(ndim, shape):
        return pl.BlockSpec(shape, lambda i: (0,) * ndim)

    last = cx // LANES - 1
    send, tgt, hi_p, lo_p, edge_p = pl.pallas_call(
        functools.partial(prep_kernel, owners),
        out_shape=(
            sds((owners, STEPS * CAP, n_cols), F32),
            sds((owners, 1, LANES), F32),
            sds((cy, 2 * LANES), F32),
            sds((cy, LANES), F32),
            sds((STEPS, cy), F32),
        ),
        grid=(1,),
        in_specs=[
            whole(2, row_dest.shape), whole(2, row_coarse.shape), whole(3, parent_vals.shape),
            pl.BlockSpec((cy, LANES), lambda i: (0, 0)),
            pl.BlockSpec((cy, LANES), lambda i: (0, 0)),
            pl.BlockSpec((cy, LANES), lambda i: (0, 0)),
            pl.BlockSpec((cy, LANES), lambda i: (0, 0)),
            pl.BlockSpec((cy, LANES), lambda i: (0, last)),
            pl.BlockSpec((STEPS, cy, LANES), lambda i: (0, 0, 0)),
            pl.BlockSpec((STEPS, cy, LANES), lambda i: (0, 0, last)),
            whole(2, edge_owner.shape), whole(3, edge_panels.shape),
        ],
        name="prep",
    )(row_dest, row_coarse, parent_vals, elevation, flux_x, flux_y, depth, depth, wet_mask,
      wet_mask, edge_owner, edge_panels)

    n_halo = 16
    wet_hi = [round_up(w, PAD) for w in WET_HI]
    dma = pltpu.SemaphoreType.DMA
    halos = pl.pallas_call(
        functools.partial(comm_kernel, ny, nx, n_halo),
        out_shape=(
            sds((3, STATE_HI, cx), F32), sds((wet_hi[0], cx), F32),
            *[sds((w, cx), I32) for w in wet_hi],
            sds((PAD, cx), F32), sds((STEPS, PAD, cx), I32),
            sds((PAD + cy + STATE_HI, 2 * LANES), F32),
            sds((PAD + cy + STATE_HI, LANES), F32),
            sds((9, STEPS, n_coarse, n_cols), F32),
            sds((3, nx, STEPS, cy), F32),
        ),
        in_specs=[any_] * 10,
        out_specs=(any_,) * 12,
        scratch_shapes=[
            pltpu.VMEM((owners, STEPS * CAP, n_cols), F32),
            pltpu.VMEM((owners, 1, LANES), F32),
            pltpu.VMEM((STEPS, n_coarse, n_cols), F32),
            dma((2,)), dma((2,)), dma((n_halo,)), dma((n_halo,)), dma((9,)), dma((9,)),
            dma((3,)), dma((3,)), dma((1,)),
        ],
        compiler_params=pltpu.CompilerParams(has_side_effects=True),
        name="exchange",
    )(send, tgt, elevation, flux_x, flux_y, depth, wet_mask, hi_p, lo_p, edge_p)

    width = cx + LANES
    rows = PAD + cy + STATE_HI
    ext_rows = rows + PAD
    win = cy + 2 * PAD
    return pl.pallas_call(
        functools.partial(step_kernel, ny, nx),
        out_shape=(sds((cy, cx), F32),) * 3,
        in_specs=[sm] + [any_] * 17,
        out_specs=(vm,) * 3,
        scratch_shapes=[
            pltpu.VMEM((3, ext_rows, width), F32),
            pltpu.VMEM((ext_rows, width), F32),
            pltpu.VMEM((STEPS, ext_rows, width), I32),
            pltpu.VMEM((rows, 2 * LANES), F32),
            pltpu.VMEM((rows, LANES), F32),
            pltpu.VMEM((3, nx, STEPS, cy), F32),
            pltpu.VMEM((9, STEPS, n_coarse, n_cols), F32),
            pltpu.VMEM((5, win + 2 * PAD, width), F32),
            pltpu.VMEM((3, win, width), F32),
            pltpu.VMEM((win, width), F32),
            dma((32,)),
        ],
        compiler_params=pltpu.CompilerParams(vmem_limit_bytes=56 * 1024 * 1024),
        name="steps",
    )(shifts, elevation, flux_x, flux_y, depth, wet_mask, *halos)


def solution(mesh):
    in_specs = (
        P("ny", "nx"),
        P("ny", "nx"),
        P("ny", "nx"),
        P("ny", "nx"),
        P(None, "ny", "nx"),
        P(),
        P(None, ("ny", "nx"), None),
        P(None, ("ny", "nx")),
        P(None, ("ny", "nx")),
        P(None, "ny"),
        P(None, "nx", "ny"),
    )
    out_specs = (P("ny", "nx"), P("ny", "nx"), P("ny", "nx"))
    return jax.shard_map(local, mesh=mesh, in_specs=in_specs, out_specs=out_specs, check_vma=False)
```

profile of v0, /device:TPU:1, one launch (start us, length us, event | category | flops | bytes accessed | tf_op | source)
XLA Modules:
  0.0 75.1 jit_solution(10323027937855226626)
XLA Ops:
  0.6 1.3 %copy.15.shifts = s32[4,2]{1,0:T(4,128)} copy(s32[4,2]{0,1:T(2,128)} %param.16) | data formatting | bytes 64 | tf_op args[5]
  2.0 1.3 %copy.14.eowner = s32[4,1]{1,0:T(4,128)} copy(s32[4,1]{0,1:T(1,128)} %param.20) | data formatting | bytes 32 | tf_op args[9]
  3.3 3.4 %prep.1 = (f32[32,32,128]{2,1,0:T(8,128)}, f32[32,1,128]{2,1,0:T(1,128)}, f32[144,256]{1,0:T(8,128)}, f32[144,128]{1,0:T(8,128)}, f32[4,144]{1,0:T(4,128)}) custom-call(s32[4,256]{1,0:T(4,128)} %dest.1, s32[4,256]{1,0:T(4,128)} %coarse.1, f32[4,256,128]{2,1,0:T(8,128)} %vals.1, f32[144,1152]{1,0:T(8,128)} %e.5, f32[144,1152]{1,0:T(8,128)} %u.5, ...), custom_call_target="tpu_custom_call" | custom-call | tf_op jit(solution)/shard_map/prep/pallas_call | solution.py:449
  6.7 29.3 %exchange.1 = (f32[3,40,1152]{2,1,0:T(8,128)}, f32[32,1152]{1,0:T(8,128)}, s32[32,1152]{1,0:T(8,128)}, s32[24,1152]{1,0:T(8,128)}, s32[16,1152]{1,0:T(8,128)}, /...) custom-call(f32[32,32,128]{2,1,0:T(8,128)} %get-tuple-element.20.sen, ...), custom_call_target="tpu_custom_call" | custom-call | tf_op jit(solution)/shard_map/exchange/pallas_call | solution.py:477
  36.0 39.1 %steps.1 = (f32[144,1152]{1,0:T(8,128)}, f32[144,1152]{1,0:T(8,128)}, f32[144,1152]{1,0:T(8,128)}) custom-call(s32[4,2]{1,0:T(4,128)} %copy.15.shifts, f32[144,1152]{1,0:T(8,128)} %e.5, f32[144,1152]{1,0:T(8,128)} %u.5, f32[144,1152]{1,0:T(8,128)} %v.5, f32[144,1152]{1,0:T(8,128)} %depth.3, s32[4,144,1152]{2,1,0:T(8,128)} %wet.3, ...), custom_call_target="tpu_custom_call" | custom-call | tf_op jit(solution)/shard_map/steps/pallas_call | solution.py:505
where the time goes:
time: 75.3 us; the launch traced here: 75.1 us
  Pallas kernels  71.8 us (95%)
  local copies, waits for them, and re-layouts  2.64 us (4%)
    pallas_call x1, Pallas kernels, local(): pl.pallas_call(functools.partial(step_kernel, ny, nx), out_shape=(sds((cy...  39.1 us
    pallas_call x1, Pallas kernels, local(): pl.pallas_call(functools.partial(comm_kernel, ny, nx, n_halo), out_shape=...  29.3 us
    pallas_call x1, Pallas kernels, local(): pl.pallas_call(functools.partial(prep_kernel, owners), out_shape=(sds((ow...  3.42 us
    unnamed x2, local copies, waits for them, and re-layouts  2.64 us

commit v1 on v0

--- a/solution.py
+++ b/solution.py
@@ -93,8 +93,9 @@
         last = jnp.where((lane >= at) & (lane < at + AUX_LO[k]), moved, last)
     hi[:, LANES:] = second
     lo[...] = last
-    mine = eowner[...] == lax.axis_index("nx")
-    edge[...] = jnp.where(mine, epanel[:, 0, :], 0.0)
+    for s in range(STEPS):
+        mine = eowner[:, s : s + 1] == lax.axis_index("nx")
+        edge[s : s + 1, :] = jnp.where(mine, epanel[s], 0.0)
 
 
 def comm_kernel(ny, nx, n_halo, send, tgt, e, u, v, depth, wet, hi_p, lo_p, edge_p,
@@ -223,7 +224,7 @@
 
 def step_kernel(ny, nx, shifts, e, u, v, depth, wet, srs, srd, srw0, srw1, srw2, srw3,
                 nrd, nrw, hi, lo, fc, edges, out_e, out_u, out_v,
-                ext, ext_d, ext_w, hi_v, lo_v, edge_v, fc_v, work, cur, force, sems):
+                ext, ext_d, ext_w, hi_v, lo_v, edge_v, fc_v, work, cur, force, col_w, prev, sems):
     y, x = lax.axis_index("ny"), lax.axis_index("nx")
     cy, cx = e.shape
     width = ext.shape[2]
@@ -256,10 +257,9 @@
         for copy in copies[group]:
             copy.wait()
 
-    sum_r = [sum([shifts[t, 0] for t in range(s, STEPS)], jnp.int32(0)) for s in range(STEPS + 1)]
-    sum_c = [sum([shifts[t, 1] for t in range(s, STEPS)], jnp.int32(0)) for s in range(STEPS + 1)]
-
-    finish(0)
+    sum_r = [sum([shifts[0, t] for t in range(s, STEPS)], jnp.int32(0)) for s in range(STEPS + 1)]
+    sum_c = [sum([shifts[1, t] for t in range(s, STEPS)], jnp.int32(0)) for s in range(STEPS + 1)]
+
     n_coarse, n_cols = fc.shape[2], fc.shape[3]
     has_y = {-1: y > 0, 0: y >= 0, 1: y < ny - 1}
     has_x = {-1: x > 0, 0: x >= 0, 1: x < nx - 1}
@@ -272,6 +272,19 @@
         inside = (inner >= 0) & (inner < fine_count)
         return jnp.where(inside, weight, 0).astype(F32).astype(BF16)
 
+    tiles = width // LANES
+    lane = iota((PAD, LANES), 1)
+    row = iota((PAD, LANES), 0)
+
+    q = iota((2 * n_cols, LANES), 0)
+    at_q = q - jnp.where(q >= n_cols, n_cols, 0)
+    which_q = jnp.where(q < n_cols, 0, jnp.where(at_q < n_cols // 2, 1, -1))
+    lane_q = iota((2 * n_cols, LANES), 1)
+    for k in range(tiles):
+        fine = lane_q + k * LANES
+        fine = fine - jnp.where(fine >= width - PAD, width, 0)
+        col_w[:, k * LANES : (k + 1) * LANES] = weights(fine, which_q, at_q, cx, n_cols)
+    finish(0)
     lane_e = iota((n_coarse, n_cols), 1)
     row_e = iota((n_coarse, n_cols), 0)
 
@@ -295,16 +308,11 @@
         section = jnp.zeros((win, 2 * n_cols), F32)
         for piece in pieces(coarse):
             section = section + jnp.dot(row_w, piece, preferred_element_type=F32)
-        q = iota((2 * n_cols, width), 0)
-        at = q - jnp.where(q >= n_cols, n_cols, 0)
-        which = jnp.where(q < n_cols, 0, jnp.where(at < n_cols // 2, 1, -1))
-        lane = iota((2 * n_cols, width), 1)
-        fine = lane - jnp.where(lane >= width - PAD, width, 0) + sum_c[s + 1]
-        col_w = weights(fine, which, at, cx, n_cols)
+        section = section * (1.0 / (4.0 * RATIO * RATIO))
         total = jnp.zeros((win, width), F32)
         for piece in pieces(section):
-            total = total + jnp.dot(piece, col_w, preferred_element_type=F32)
-        force[...] = total * (1.0 / (4.0 * RATIO * RATIO))
+            total = total + jnp.dot(piece, col_w[...], preferred_element_type=F32)
+        force[...] = total
 
     rows_here = hi_v.shape[0]
     lane_t = iota((rows_here, LANES), 1)
@@ -326,16 +334,34 @@
         else:
             ext_w[k - 1, pl.ds(0, rows_here), cx : cx + LANES] = tile.astype(I32)
 
-    def rows_at(load, start):
+    edge_sum = jnp.sum(edge_v[...], axis=1)
+
+    def across(pieces_, by):
+        turned = [pltpu.roll(f, lax.rem(LANES - by, LANES), 1) for f in pieces_]
+        keep = lane < LANES - by
+        return [jnp.where(keep, turned[k], turned[(k + 1) % tiles]) for k in range(tiles)]
+
+    def window(load, start, by):
         base = pl.multiple_of(start // PAD * PAD, PAD)
-        both = load(pl.ds(base, 2 * PAD))
-        return pltpu.roll(both, lax.rem(2 * PAD - (start - base), 2 * PAD), 0)[:PAD]
-
-    lane = iota((PAD, width), 1)
-    row = iota((PAD, width), 0)
-    row_1 = iota((PAD, 1), 0)
-    col_local = lane - jnp.where(lane >= width - PAD, width, 0)
-    edge_sum = jnp.sum(edge_v[...], axis=1)
+        off = start - base
+        turn = lax.rem(PAD - off, PAD)
+        upper = row >= off
+        out = []
+        for k in range(tiles):
+            cols = pl.ds(k * LANES, LANES)
+            both = jnp.where(upper, load(pl.ds(base, PAD), cols),
+                             load(pl.ds(pl.multiple_of(base + PAD, PAD), PAD), cols))
+            out.append(pltpu.roll(both, turn, 0))
+        return across(out, by)
+
+    def faces(low, up, normal, cross):
+        opened = low[3] * up[3]
+        thin = 0.25 * opened
+        n_l, n_h = low[normal], up[normal]
+        mass = thin * (2.0 * (n_l + n_h) - (up[0] - low[0]))
+        push = thin * ((low[4] + up[4]) * (up[0] + low[0]) - (n_h - n_l))
+        shear = thin * (low[cross] - up[cross])
+        return mass, push, shear
 
     for s in range(STEPS):
         forcing(s)
@@ -343,91 +369,126 @@
             finish(1)
         finish(2 + s)
         off_r, off_c = sum_r[s + 1], sum_c[s + 1]
-        gcol = col_local + (x * cx + off_c)
-        col_in = (gcol >= 0) & (gcol < nx * cx)
-        col_ok = col_in & (gcol + shifts[s, 1] < nx * cx)
-        ghost_col = gcol == -1
-        back = lax.rem(width - off_c, width)
-        back_0 = lax.rem(width - sum_c[0], width)
         edge_rows = [edge_sum[d, s : s + 1, :] for d in range(3)]
 
         def fill(t, carry):
             a = pl.multiple_of(t * PAD, PAD)
-            local = row + (a - PAD) + off_r
-            grow = local + y * cy
+            here_rows = pl.ds(a, PAD)
+            grow = row + (a - PAD) + off_r + y * cy
             row_in = (grow >= 0) & (grow < ny * cy)
-            inside = row_in & col_in
-            valid = row_in & col_ok & (grow + shifts[s, 0] < ny * cy)
-            fields = []
-            for k in range(3):
-                if s == 0:
-                    piece = rows_at(lambda at: ext[k, at, :], a - PAD + sum_r[0])
-                    piece = pltpu.roll(piece, back_0, 1)
+            row_ok = row_in & (grow + shifts[0, s] < ny * cy)
+            if s == 0:
+                fields = [
+                    window(lambda r, c: ext[k, r, c], a - PAD + sum_r[0], sum_c[0])
+                    for k in range(3)
+                ]
+            else:
+                fields = [
+                    [cur[k, here_rows, m * LANES : (m + 1) * LANES] for m in range(tiles)]
+                    for k in range(3)
+                ]
+            wets = window(lambda r, c: ext_w[s, r, c], a + off_r, off_c)
+            beds = window(lambda r, c: ext_d[r, c], a + off_r, off_c)
+            added = across(
+                [force[here_rows, m * LANES : (m + 1) * LANES] for m in range(tiles)], off_c)
+            for m in range(tiles):
+                valid, inside = row_ok, row_in
+                local_col = lane + m * LANES
+                if m == tiles - 1:
+                    local_col = local_col - jnp.where(local_col >= width - PAD, width, 0)
+                gcol = local_col + (x * cx + off_c)
+                if (m + 1) * LANES > cx - STEPS * SH:
+                    inside = inside & (gcol >= 0) & (gcol < nx * cx)
+                    valid = valid & (gcol >= 0) & (gcol + shifts[1, s] < nx * cx)
+                e_m = jnp.where(valid, fields[0][m], 0.0) + added[m]
+                e_m = jnp.where(inside, e_m, 0.0)
+                u_m = jnp.where(valid, fields[1][m], 0.0)
+                v_m = jnp.where(valid, fields[2][m], 0.0)
+                w_m = jnp.where(inside, wets[m].astype(F32), 0.0)
+                b_m = jnp.where(inside, beds[m], 0.0)
+                if m == tiles - 1:
+                    spot = iota((PAD, cy), 0) + (a - PAD) + off_r
+                    at = iota((PAD, cy), 1)
+                    value = jnp.zeros((PAD, cy), F32)
+                    for d in range(3):
+                        value = value + jnp.where(at + (d - 1) * cy == spot, edge_rows[d], 0.0)
+                    value = jnp.sum(value, axis=1, keepdims=True)
+                    ghost = (gcol == -1) & row_in
+                    e_m = jnp.where(ghost, value, e_m)
+                    w_m = jnp.where(ghost, 1.0, w_m)
+                for k, field in enumerate((e_m, u_m, v_m, w_m, b_m)):
+                    work[k, here_rows, m * LANES : (m + 1) * LANES] = field
+            return carry
+
+        lax.fori_loop(0, win // PAD, fill, 0)
+        last_step = s == STEPS - 1
+
+        def advance(t, keep_result):
+            a = pl.multiple_of(t * PAD, PAD)
+            rows_a = pl.ds(a, PAD)
+            rows_b = pl.ds(pl.multiple_of(a + PAD, PAD), PAD)
+
+            def at(k, rows_, m):
+                return work[k, rows_, m * LANES : (m + 1) * LANES]
+
+            def turned_west(m):
+                return [pltpu.roll(at(k, rows_a, m), LANES - 1, 1) for k in range(5)]
+
+            def x_faces(here, own, nxt):
+                east = [jnp.where(lane < LANES - 1, p, q) for p, q in zip(own, nxt)]
+                return faces(here, east, 1, 2)
+
+            n_out = tiles - 1 if last_step else tiles
+            first = turned_west(0)
+            tail = [at(k, rows_a, tiles - 1) for k in range(5)]
+            flux_tail = x_faces(tail, turned_west(tiles - 1), first)
+            before = [pltpu.roll(f, 1, 1) for f in flux_tail]
+            own = first
+            for m in range(n_out):
+                here = [at(k, rows_a, m) for k in range(5)]
+                if m == tiles - 1:
+                    flux = flux_tail
                 else:
-                    piece = cur[k, pl.ds(a, PAD), :]
-                fields.append(jnp.where(valid, piece, 0.0))
-            surface = jnp.where(inside, fields[0] + force[pl.ds(a, PAD), :], 0.0)
-            mask = rows_at(lambda at: ext_w[s, at, :], a + off_r)
-            mask = jnp.where(inside, pltpu.roll(mask, back, 1).astype(F32), 0.0)
-            bed = rows_at(lambda at: ext_d[at, :], a + off_r)
-            bed = jnp.where(inside, pltpu.roll(bed, back, 1), 0.0)
-            spot = row_1 + (a - PAD) + off_r
-            value = jnp.zeros((PAD, 1), F32)
-            for d in range(3):
-                at = iota((PAD, cy), 1) + (d - 1) * cy
-                value = value + jnp.sum(
-                    jnp.where(at == spot, edge_rows[d], 0.0), axis=1, keepdims=True)
-            ghost = ghost_col & row_in
-            surface = jnp.where(ghost, value, surface)
-            mask = jnp.where(ghost, 1.0, mask)
-            for k, field in enumerate((surface, fields[1], fields[2], mask, bed)):
-                work[k, pl.ds(a + PAD, PAD), :] = field
+                    nxt = turned_west(m + 1)
+                    flux = x_faces(here, own, nxt)
+                    own = nxt
+                turned = [pltpu.roll(f, 1, 1) for f in flux]
+                d_x = [f - jnp.where(lane >= 1, p, q) for f, p, q in zip(flux, turned, before)]
+                before = turned
+                upper = [
+                    pltpu.roll(jnp.where(row >= 1, here[k], at(k, rows_b, m)), PAD - 1, 0)
+                    for k in range(5)
+                ]
+                north = faces(here, upper, 2, 1)
+                cols = pl.ds(m * LANES, LANES)
+                d_y = []
+                for k in range(3):
+                    south = jnp.where(row < PAD - 1, north[k], prev[k, :, cols])
+                    d_y.append(north[k] - pltpu.roll(south, 1, 0))
+                    prev[k, :, cols] = north[k]
+                if not keep_result:
+                    continue
+                new = (
+                    here[0] - 0.25 * (d_x[0] + d_y[0]),
+                    here[3] * (here[1] - 0.25 * (d_x[1] + d_y[2])),
+                    here[3] * (here[2] - 0.25 * (d_x[2] + d_y[1])),
+                )
+                for k in range(3):
+                    if last_step:
+                        rows_o = pl.ds(pl.multiple_of(a - PAD, PAD), PAD)
+                        (out_e, out_u, out_v)[k][rows_o, cols] = new[k]
+                    else:
+                        cur[k, rows_a, cols] = new[k]
+
+        def body(t, carry):
+            advance(t, True)
             return carry
 
-        lax.fori_loop(0, win // PAD, fill, 0)
-
-        def advance(t, carry):
-            a = pl.multiple_of(t * PAD, PAD)
-            around = [work[k, pl.ds(a, 3 * PAD), :] for k in range(5)]
-            here = [f[PAD : 2 * PAD] for f in around]
-
-            def faces(low, up, normal, cross):
-                e_l, m_l, b_l = low[0], low[3], low[4]
-                e_h, m_h, b_h = up[0], up[3], up[4]
-                opened = m_l * m_h
-                thin = 0.25 * opened
-                rise = e_h - e_l
-                level = e_h + e_l
-                n_l, n_h = low[normal], up[normal]
-                mass = thin * (2.0 * (n_l + n_h) - rise)
-                push = thin * ((b_l + b_h) * level - (n_h - n_l))
-                shear = thin * (low[cross] - up[cross])
-                return mass, push, shear
-
-            east = [pltpu.roll(f, width - 1, 1) for f in here]
-            flux = faces(here, east, 1, 2)
-            total = [f - pltpu.roll(f, 1, 1) for f in flux]
-            upper = [f[PAD + 1 : 2 * PAD + 1] for f in around]
-            lower = [f[PAD - 1 : 2 * PAD - 1] for f in around]
-            f_n = faces(here, upper, 2, 1)
-            f_s = faces(lower, here, 2, 1)
-            d_mass, d_push, d_shear = [p - q for p, q in zip(f_n, f_s)]
-            new = (
-                here[0] - 0.25 * (total[0] + d_mass),
-                here[3] * (here[1] - 0.25 * (total[1] + d_shear)),
-                here[3] * (here[2] - 0.25 * (total[2] + d_push)),
-            )
-            for k in range(3):
-                if s == STEPS - 1:
-                    (out_e, out_u, out_v)[k][pl.ds(pl.multiple_of(a - PAD, PAD), PAD), :] = new[k][:, :cx]
-                else:
-                    cur[k, pl.ds(a, PAD), :] = new[k]
-            return carry
-
-        if s == STEPS - 1:
-            lax.fori_loop(1, 1 + cy // PAD, advance, 0)
+        if last_step:
+            advance(0, False)
+            lax.fori_loop(1, 1 + cy // PAD, body, 0)
         else:
-            lax.fori_loop(0, win // PAD, advance, 0)
+            lax.fori_loop(0, win // PAD, body, 0)
 
 
 def local(elevation, flux_x, flux_y, depth, wet_mask, shifts, parent_vals, row_dest, row_coarse,
@@ -465,11 +526,11 @@
             pl.BlockSpec((cy, LANES), lambda i: (0, last)),
             pl.BlockSpec((STEPS, cy, LANES), lambda i: (0, 0, 0)),
             pl.BlockSpec((STEPS, cy, LANES), lambda i: (0, 0, last)),
-            whole(2, edge_owner.shape), whole(3, edge_panels.shape),
+            whole(2, edge_owner.shape[::-1]), whole(3, edge_panels.shape),
         ],
         name="prep",
     )(row_dest, row_coarse, parent_vals, elevation, flux_x, flux_y, depth, depth, wet_mask,
-      wet_mask, edge_owner, edge_panels)
+      wet_mask, edge_owner.T, edge_panels)
 
     n_halo = 16
     wet_hi = [round_up(w, PAD) for w in WET_HI]
@@ -515,14 +576,16 @@
             pltpu.VMEM((rows, LANES), F32),
             pltpu.VMEM((3, nx, STEPS, cy), F32),
             pltpu.VMEM((9, STEPS, n_coarse, n_cols), F32),
-            pltpu.VMEM((5, win + 2 * PAD, width), F32),
+            pltpu.VMEM((5, win + PAD, width), F32),
             pltpu.VMEM((3, win, width), F32),
             pltpu.VMEM((win, width), F32),
+            pltpu.VMEM((2 * n_cols, width), BF16),
+            pltpu.VMEM((3, PAD, width), F32),
             dma((32,)),
         ],
         compiler_params=pltpu.CompilerParams(vmem_limit_bytes=56 * 1024 * 1024),
         name="steps",
-    )(shifts, elevation, flux_x, flux_y, depth, wet_mask, *halos)
+    )(shifts.T, elevation, flux_x, flux_y, depth, wet_mask, *halos)
 
 
 def solution(mesh):

time: 75.3 us -> 69.4 us (0.922)
  Pallas kernels: 71.8 us -> 68.6 us
  local copies, waits for them, and re-layouts: 2.64 us -> 0 us
    pallas_call x1, Pallas kernels: 39.1 us -> 35.8 us  [local(): pl.pallas_call(functools.partial(step_kernel, ny, nx), out_shape=(sds((cy...]
    unnamed x2 -> x0, local copies, waits for them, and re-layouts: 2.64 us -> none
where the time goes in v1:
time: 69.4 us; the launch traced here: 69.2 us
  Pallas kernels  68.6 us (99%)
    pallas_call x1, Pallas kernels, local(): pl.pallas_call(functools.partial(step_kernel, ny, nx), out_shape=(sds((cy...  35.8 us
    pallas_call x1, Pallas kernels, local(): pl.pallas_call(functools.partial(comm_kernel, ny, nx, n_halo), out_shape=...  29.3 us
    pallas_call x1, Pallas kernels, local(): pl.pallas_call(functools.partial(prep_kernel, owners), out_shape=(sds((ow...  3.44 us

profile of v1, /device:TPU:1, one launch (start us, length us, event | category | flops | bytes accessed | tf_op | source)
XLA Modules:
  0.0 69.2 jit_solution(10912568527752398746)
XLA Ops:
  0.6 3.4 %prep.1 = (f32[32,32,128]{2,1,0:T(8,128)}, f32[32,1,128]{2,1,0:T(1,128)}, f32[144,256]{1,0:T(8,128)}, f32[144,128]{1,0:T(8,128)}, f32[4,144]{1,0:T(4,128)}) custom-call(s32[4,256]{1,0:T(4,128)} %dest.1, s32[4,256]{1,0:T(4,128)} %coarse.1, f32[4,256,128]{2,1,0:T(8,128)} %vals.1, f32[144,1152]{1,0:T(8,128)} %e.5, f32[144,1152]{1,0:T(8,128)} %u.5, ...), custom_call_target="tpu_custom_call" | custom-call | tf_op jit(solution)/shard_map/prep/pallas_call | solution.py:510
  4.1 29.3 %exchange.1 = (f32[3,40,1152]{2,1,0:T(8,128)}, f32[32,1152]{1,0:T(8,128)}, s32[32,1152]{1,0:T(8,128)}, s32[24,1152]{1,0:T(8,128)}, s32[16,1152]{1,0:T(8,128)}, /...) custom-call(f32[32,32,128]{2,1,0:T(8,128)} %get-tuple-element.20.sen, ...), custom_call_target="tpu_custom_call" | custom-call | tf_op jit(solution)/shard_map/exchange/pallas_call | solution.py:538
  33.4 35.8 %steps.1 = (f32[144,1152]{1,0:T(8,128)}, f32[144,1152]{1,0:T(8,128)}, f32[144,1152]{1,0:T(8,128)}) custom-call(s32[2,4]{1,0:T(2,128)} %bitcast.2, f32[144,1152]{1,0:T(8,128)} %e.5, f32[144,1152]{1,0:T(8,128)} %u.5, f32[144,1152]{1,0:T(8,128)} %v.5, f32[144,1152]{1,0:T(8,128)} %depth.3, s32[4,144,1152]{2,1,0:T(8,128)} %wet.3, ...), custom_call_target="tpu_custom_call" | custom-call | tf_op jit(solution)/shard_map/steps/pallas_call | solution.py:566

commit v2 on v1

--- a/solution.py
+++ b/solution.py
@@ -355,10 +355,9 @@
         return across(out, by)
 
     def faces(low, up, normal, cross):
-        opened = low[3] * up[3]
-        thin = 0.25 * opened
+        thin = low[3] * up[3]
         n_l, n_h = low[normal], up[normal]
-        mass = thin * (2.0 * (n_l + n_h) - (up[0] - low[0]))
+        mass = thin * ((n_l + n_h) - (up[0] - low[0]))
         push = thin * ((low[4] + up[4]) * (up[0] + low[0]) - (n_h - n_l))
         shear = thin * (low[cross] - up[cross])
         return mass, push, shear
@@ -404,8 +403,10 @@
                 e_m = jnp.where(inside, e_m, 0.0)
                 u_m = jnp.where(valid, fields[1][m], 0.0)
                 v_m = jnp.where(valid, fields[2][m], 0.0)
-                w_m = jnp.where(inside, wets[m].astype(F32), 0.0)
-                b_m = jnp.where(inside, beds[m], 0.0)
+                if s == 0:
+                    u_m, v_m = 2.0 * u_m, 2.0 * v_m
+                w_m = jnp.where(inside, 0.25 * wets[m].astype(F32), 0.0)
+                b_m = jnp.where(inside, 2.0 * beds[m], 0.0)
                 if m == tiles - 1:
                     spot = iota((PAD, cy), 0) + (a - PAD) + off_r
                     at = iota((PAD, cy), 1)
@@ -415,21 +416,23 @@
                     value = jnp.sum(value, axis=1, keepdims=True)
                     ghost = (gcol == -1) & row_in
                     e_m = jnp.where(ghost, value, e_m)
-                    w_m = jnp.where(ghost, 1.0, w_m)
+                    w_m = jnp.where(ghost, 0.25, w_m)
                 for k, field in enumerate((e_m, u_m, v_m, w_m, b_m)):
-                    work[k, here_rows, m * LANES : (m + 1) * LANES] = field
+                    work[k, m, here_rows, :] = field
             return carry
 
-        lax.fori_loop(0, win // PAD, fill, 0)
+        lax.fori_loop(0, win // PAD, fill, 0, unroll=2)
         last_step = s == STEPS - 1
 
         def advance(t, keep_result):
             a = pl.multiple_of(t * PAD, PAD)
             rows_a = pl.ds(a, PAD)
-            rows_b = pl.ds(pl.multiple_of(a + PAD, PAD), PAD)
+            rows_n = pl.ds(a + 1, PAD)
+            rows_f = pl.ds(pl.multiple_of(a + PAD, PAD), PAD)
+            rows_s = pl.ds(a + PAD - 1, PAD)
 
             def at(k, rows_, m):
-                return work[k, rows_, m * LANES : (m + 1) * LANES]
+                return work[k, m, rows_, :]
 
             def turned_west(m):
                 return [pltpu.roll(at(k, rows_a, m), LANES - 1, 1) for k in range(5)]
@@ -455,23 +458,19 @@
                 turned = [pltpu.roll(f, 1, 1) for f in flux]
                 d_x = [f - jnp.where(lane >= 1, p, q) for f, p, q in zip(flux, turned, before)]
                 before = turned
-                upper = [
-                    pltpu.roll(jnp.where(row >= 1, here[k], at(k, rows_b, m)), PAD - 1, 0)
-                    for k in range(5)
-                ]
-                north = faces(here, upper, 2, 1)
+                north = faces(here, [at(k, rows_n, m) for k in range(5)], 2, 1)
                 cols = pl.ds(m * LANES, LANES)
                 d_y = []
                 for k in range(3):
-                    south = jnp.where(row < PAD - 1, north[k], prev[k, :, cols])
-                    d_y.append(north[k] - pltpu.roll(south, 1, 0))
-                    prev[k, :, cols] = north[k]
+                    prev[k, m, rows_f, :] = north[k]
+                    d_y.append(north[k] - prev[k, m, rows_s, :])
                 if not keep_result:
                     continue
+                scale = (2.0 if last_step else 4.0) * here[3]
                 new = (
-                    here[0] - 0.25 * (d_x[0] + d_y[0]),
-                    here[3] * (here[1] - 0.25 * (d_x[1] + d_y[2])),
-                    here[3] * (here[2] - 0.25 * (d_x[2] + d_y[1])),
+                    here[0] - (d_x[0] + d_y[0]),
+                    scale * (here[1] - (d_x[1] + d_y[2])),
+                    scale * (here[2] - (d_x[2] + d_y[1])),
                 )
                 for k in range(3):
                     if last_step:
@@ -576,11 +575,11 @@
             pltpu.VMEM((rows, LANES), F32),
             pltpu.VMEM((3, nx, STEPS, cy), F32),
             pltpu.VMEM((9, STEPS, n_coarse, n_cols), F32),
-            pltpu.VMEM((5, win + PAD, width), F32),
+            pltpu.VMEM((5, width // LANES, win + PAD, LANES), F32),
             pltpu.VMEM((3, win, width), F32),
             pltpu.VMEM((win, width), F32),
             pltpu.VMEM((2 * n_cols, width), BF16),
-            pltpu.VMEM((3, PAD, width), F32),
+            pltpu.VMEM((3, width // LANES, win + PAD, LANES), F32),
             dma((32,)),
         ],
         compiler_params=pltpu.CompilerParams(vmem_limit_bytes=56 * 1024 * 1024),

time: 69.4 us -> 65.8 us (0.948)
  Pallas kernels: 68.6 us -> 65.1 us
    pallas_call x1, Pallas kernels: 35.8 us -> 32.3 us  [local(): pl.pallas_call(functools.partial(step_kernel, ny, nx), out_shape=(sds((cy...]
where the time goes in v2:
time: 65.8 us; the launch traced here: 65.7 us
  Pallas kernels  65.1 us (99%)
    pallas_call x1, Pallas kernels, local(): pl.pallas_call(functools.partial(step_kernel, ny, nx), out_shape=(sds((cy...  32.3 us
    pallas_call x1, Pallas kernels, local(): pl.pallas_call(functools.partial(comm_kernel, ny, nx, n_halo), out_shape=...  29.3 us
    pallas_call x1, Pallas kernels, local(): pl.pallas_call(functools.partial(prep_kernel, owners), out_shape=(sds((ow...  3.44 us

profile of v2, /device:TPU:1, one launch (start us, length us, event | category | flops | bytes accessed | tf_op | source)
XLA Modules:
  0.0 65.7 jit_solution(9433017328946119152)
XLA Ops:
  0.6 3.4 %prep.1 = (f32[32,32,128]{2,1,0:T(8,128)}, f32[32,1,128]{2,1,0:T(1,128)}, f32[144,256]{1,0:T(8,128)}, f32[144,128]{1,0:T(8,128)}, f32[4,144]{1,0:T(4,128)}) custom-call(s32[4,256]{1,0:T(4,128)} %dest.1, s32[4,256]{1,0:T(4,128)} %coarse.1, f32[4,256,128]{2,1,0:T(8,128)} %vals.1, f32[144,1152]{1,0:T(8,128)} %e.5, f32[144,1152]{1,0:T(8,128)} %u.5, ...), custom_call_target="tpu_custom_call" | custom-call | tf_op jit(solution)/shard_map/prep/pallas_call | solution.py:509
  4.1 29.3 %exchange.1 = (f32[3,40,1152]{2,1,0:T(8,128)}, f32[32,1152]{1,0:T(8,128)}, s32[32,1152]{1,0:T(8,128)}, s32[24,1152]{1,0:T(8,128)}, s32[16,1152]{1,0:T(8,128)}, /...) custom-call(f32[32,32,128]{2,1,0:T(8,128)} %get-tuple-element.20.sen, ...), custom_call_target="tpu_custom_call" | custom-call | tf_op jit(solution)/shard_map/exchange/pallas_call | solution.py:537
  33.4 32.3 %steps.1 = (f32[144,1152]{1,0:T(8,128)}, f32[144,1152]{1,0:T(8,128)}, f32[144,1152]{1,0:T(8,128)}) custom-call(s32[2,4]{1,0:T(2,128)} %bitcast.2, f32[144,1152]{1,0:T(8,128)} %e.5, f32[144,1152]{1,0:T(8,128)} %u.5, f32[144,1152]{1,0:T(8,128)} %v.5, f32[144,1152]{1,0:T(8,128)} %depth.3, s32[4,144,1152]{2,1,0:T(8,128)} %wet.3, ...), custom_call_target="tpu_custom_call" | custom-call | tf_op jit(solution)/shard_map/steps/pallas_call | solution.py:565

commit v3 on v2

--- a/solution.py
+++ b/solution.py
@@ -98,9 +98,10 @@
         edge[s : s + 1, :] = jnp.where(mine, epanel[s], 0.0)
 
 
-def comm_kernel(ny, nx, n_halo, send, tgt, e, u, v, depth, wet, hi_p, lo_p, edge_p,
+def comm_kernel(ny, nx, n_halo, dest, coarse_in, vals, e_0, u_0, v_0, d_0, d_1, w_0, w_1, eowner,
+                epanel, e, u, v, depth, wet,
                 srs, srd, srw0, srw1, srw2, srw3, nrd, nrw, hi, lo, fc, edges,
-                got, got_t, own, a_ssem, a_rsem, h_ssem, h_rsem, f_ssem, f_rsem,
+                send, tgt, hi_p, lo_p, edge_p, got, got_t, own, a_ssem, a_rsem, h_ssem, h_rsem, f_ssem, f_rsem,
                 e_ssem, e_rsem, l_sem):
     y, x = lax.axis_index("ny"), lax.axis_index("nx")
     owners = ny * nx
@@ -122,12 +123,6 @@
         for copy in to_owner(k):
             copy.start()
         return carry
-
-    lax.fori_loop(1, owners, start_owner, 0)
-    self_v = pltpu.make_async_copy(send.at[me], got.at[me], a_rsem.at[0])
-    self_t = pltpu.make_async_copy(tgt.at[me], got_t.at[me], a_rsem.at[1])
-    self_v.start()
-    self_t.start()
 
     def sends_to(dy, dx):
         terms = []
@@ -155,6 +150,14 @@
     assert len(plan) == n_halo
     halos = []
     for k, (dy, dx, src, dst) in enumerate(plan):
+        if dx and not plan[k - 1][1]:
+            prep_kernel(owners, dest, coarse_in, vals, e_0, u_0, v_0, d_0, d_1, w_0, w_1, eowner,
+                        epanel, send, tgt, hi_p, lo_p, edge_p)
+            lax.fori_loop(1, owners, start_owner, 0)
+            self_v = pltpu.make_async_copy(send.at[me], got.at[me], a_rsem.at[0])
+            self_t = pltpu.make_async_copy(tgt.at[me], got_t.at[me], a_rsem.at[1])
+            self_v.start()
+            self_t.start()
         copy = remote(src, dst, h_ssem.at[k], h_rsem.at[k], y + dy, x + dx)
         halos.append((copy, dy, dx))
         pl.when(sends_to(dy, dx))(copy.start)
@@ -506,31 +509,6 @@
         return pl.BlockSpec(shape, lambda i: (0,) * ndim)
 
     last = cx // LANES - 1
-    send, tgt, hi_p, lo_p, edge_p = pl.pallas_call(
-        functools.partial(prep_kernel, owners),
-        out_shape=(
-            sds((owners, STEPS * CAP, n_cols), F32),
-            sds((owners, 1, LANES), F32),
-            sds((cy, 2 * LANES), F32),
-            sds((cy, LANES), F32),
-            sds((STEPS, cy), F32),
-        ),
-        grid=(1,),
-        in_specs=[
-            whole(2, row_dest.shape), whole(2, row_coarse.shape), whole(3, parent_vals.shape),
-            pl.BlockSpec((cy, LANES), lambda i: (0, 0)),
-            pl.BlockSpec((cy, LANES), lambda i: (0, 0)),
-            pl.BlockSpec((cy, LANES), lambda i: (0, 0)),
-            pl.BlockSpec((cy, LANES), lambda i: (0, 0)),
-            pl.BlockSpec((cy, LANES), lambda i: (0, last)),
-            pl.BlockSpec((STEPS, cy, LANES), lambda i: (0, 0, 0)),
-            pl.BlockSpec((STEPS, cy, LANES), lambda i: (0, 0, last)),
-            whole(2, edge_owner.shape[::-1]), whole(3, edge_panels.shape),
-        ],
-        name="prep",
-    )(row_dest, row_coarse, parent_vals, elevation, flux_x, flux_y, depth, depth, wet_mask,
-      wet_mask, edge_owner.T, edge_panels)
-
     n_halo = 16
     wet_hi = [round_up(w, PAD) for w in WET_HI]
     dma = pltpu.SemaphoreType.DMA
@@ -545,9 +523,25 @@
             sds((9, STEPS, n_coarse, n_cols), F32),
             sds((3, nx, STEPS, cy), F32),
         ),
-        in_specs=[any_] * 10,
+        grid=(1,),
+        in_specs=[
+            whole(2, row_dest.shape), whole(2, row_coarse.shape), whole(3, parent_vals.shape),
+            pl.BlockSpec((cy, LANES), lambda i: (0, 0)),
+            pl.BlockSpec((cy, LANES), lambda i: (0, 0)),
+            pl.BlockSpec((cy, LANES), lambda i: (0, 0)),
+            pl.BlockSpec((cy, LANES), lambda i: (0, 0)),
+            pl.BlockSpec((cy, LANES), lambda i: (0, last)),
+            pl.BlockSpec((STEPS, cy, LANES), lambda i: (0, 0, 0)),
+            pl.BlockSpec((STEPS, cy, LANES), lambda i: (0, 0, last)),
+            whole(2, edge_owner.shape[::-1]), whole(3, edge_panels.shape),
+        ] + [any_] * 5,
         out_specs=(any_,) * 12,
         scratch_shapes=[
+            pltpu.VMEM((owners, STEPS * CAP, n_cols), F32),
+            pltpu.VMEM((owners, 1, LANES), F32),
+            pltpu.VMEM((cy, 2 * LANES), F32),
+            pltpu.VMEM((cy, LANES), F32),
+            pltpu.VMEM((STEPS, cy), F32),
             pltpu.VMEM((owners, STEPS * CAP, n_cols), F32),
             pltpu.VMEM((owners, 1, LANES), F32),
             pltpu.VMEM((STEPS, n_coarse, n_cols), F32),
@@ -556,7 +550,8 @@
         ],
         compiler_params=pltpu.CompilerParams(has_side_effects=True),
         name="exchange",
-    )(send, tgt, elevation, flux_x, flux_y, depth, wet_mask, hi_p, lo_p, edge_p)
+    )(row_dest, row_coarse, parent_vals, elevation, flux_x, flux_y, depth, depth, wet_mask,
+      wet_mask, edge_owner.T, edge_panels, elevation, flux_x, flux_y, depth, wet_mask)
 
     width = cx + LANES
     rows = PAD + cy + STATE_HI

time: 65.8 us -> 67.7 us (1.029)
  Pallas kernels: 65.1 us -> 66.5 us
    pallas_call x1, Pallas kernels: 29.3 us -> 34.3 us  [local(): pl.pallas_call(functools.partial(comm_kernel, ny, nx, n_halo), out_shape=...]
    pallas_call x1 -> x0, Pallas kernels: 3.44 us -> none  [local(): pl.pallas_call(functools.partial(prep_kernel, owners), out_shape=(sds((ow...]
where the time goes in v3:
time: 67.7 us; the launch traced here: 67.2 us
  Pallas kernels  66.5 us (98%)
    pallas_call x1, Pallas kernels, local(): pl.pallas_call(functools.partial(comm_kernel, ny, nx, n_halo), out_shape=...  34.3 us
    pallas_call x1, Pallas kernels, local(): pl.pallas_call(functools.partial(step_kernel, ny, nx), out_shape=(sds((cy...  32.2 us

profile of v3, /device:TPU:1, one launch (start us, length us, event | category | flops | bytes accessed | tf_op | source)
XLA Modules:
  0.0 67.2 jit_solution(3121809065080638168)
XLA Ops:
  0.6 34.3 %exchange.1 = (f32[3,40,1152]{2,1,0:T(8,128)}, f32[32,1152]{1,0:T(8,128)}, s32[32,1152]{1,0:T(8,128)}, s32[24,1152]{1,0:T(8,128)}, s32[16,1152]{1,0:T(8,128)}, /...) custom-call(s32[4,256]{1,0:T(4,128)} %dest.1, ...), custom_call_target="tpu_custom_call" | custom-call | tf_op jit(solution)/shard_map/exchange/pallas_call | solution.py:515
  34.9 32.2 %steps.1 = (f32[144,1152]{1,0:T(8,128)}, f32[144,1152]{1,0:T(8,128)}, f32[144,1152]{1,0:T(8,128)}) custom-call(s32[2,4]{1,0:T(2,128)} %bitcast.2, f32[144,1152]{1,0:T(8,128)} %e.3, f32[144,1152]{1,0:T(8,128)} %u.3, f32[144,1152]{1,0:T(8,128)} %v.3, f32[144,1152]{1,0:T(8,128)} %depth.3, s32[4,144,1152]{2,1,0:T(8,128)} %wet.3, ...), custom_call_target="tpu_custom_call" | custom-call | tf_op jit(solution)/shard_map/steps/pallas_call | solution.py:560
